TPU v7x, 32 devices: a whole 2x2x4 slice. The times are simulated.
32 devices in a mesh: sec: 8 (over y, x, core), op: 4 (over z).
Axes of the slice: x: 2, y: 2, z: 4, core: 2. Of those that a mesh axis runs over, the one named last changes fastest.
Arguments:
- psi: bfloat16 [8, 512, 512], P('sec', 'op'), may hold values from -6 to 6
- left_ops: bfloat16 [24, 8, 512, 512], P(None, 'sec', None, 'op'), may hold values from -0.0546875 to 0.0546875
- right_ops: bfloat16 [24, 8, 512, 512], P(None, 'sec', 'op'), may hold values from -0.25 to 0.25
- sources: int32 [8, 24], P('sec'), may hold values from 0 to 7
- counts: int32 [8], P('sec'), may hold values from 6 to 24, as said below
- dims_left: int32 [8], P('sec'), may hold values from 128 to 512, as said below
- dims_right: int32 [8], P('sec'), may hold values from 128 to 512, as said below
Outputs:
- sigma: bfloat16 [8, 512, 512], P('sec', 'op')
Inputs may be any that keep to these rules, and one draw needn't show every extreme that they name: `counts`: some sector has all 24 terms active. `dims_left`: some sector has the full padded dimension. `dims_right`: some sector has the full padded dimension.
All inputs are finite; a program needn't handle non-finite values.
Results may differ from a plain program's by a relative error of at most 0.0049.
Values may be sent and summed in bfloat16 or wider, within the bound.
A program may use at most 128 MiB of HBM per device.

v0:
```python
import functools

import jax
import jax.numpy as jnp
from jax import lax
from jax.experimental import pallas as pl
from jax.experimental.pallas import tpu as pltpu
from jax.sharding import PartitionSpec as P

MESH = pl.DeviceIdType.MESH


def flip(j, q):
    out, bit = 0, 1
    while bit <= q:
        out = out + ((j // bit + q // bit % 2) % 2) * bit
        bit *= 2
    return out + j // bit * bit


def kernel(n_sec, n_op, chunks, parts, psi_ref, left_hbm, right_hbm, src_ref, cnt_ref, dl_ref, dr_ref, out_ref, *scratch):
    pan, at = [], 0
    for q in range(n_op):
        pan.append(scratch[at:at + len(parts[q])])
        at += len(parts[q])
    (lv, rv, xs, xr, acc, sb, rb, local_sem, z_send, z_recv, s_send, s_recv, m_send, m_recv, x_send, x_recv,
     r_send, r_recv, near_out, near_in, far_out, far_in, near_send, near_recv, far_send, far_recv) = scratch[at:]
    s = lax.axis_index("sec")
    j = lax.axis_index("op")
    groups = n_sec // 2
    g, core = s // 2, s % 2
    mate = g * 2 + 1 - core
    rows, cols = psi_ref.shape
    terms = lv.shape[0]
    width = rv.shape[1]
    per = terms // chunks
    high = n_op // 2
    order = [high] + list(range(1, high)) + list(range(high + 1, n_op))
    paired = (0, 1, 2, 3) if n_op == 4 else ()

    load_r = pltpu.make_async_copy(right_hbm, rv, local_sem.at[0])
    load_l = pltpu.make_async_copy(left_hbm, lv, local_sem.at[1])

    def op_at(q):
        return flip(j, q)

    def from_group(d):
        return (g - d + groups) % groups

    barrier = pltpu.get_barrier_semaphore()
    for q in range(1, n_op):
        pl.semaphore_signal(barrier, inc=1, device_id={"op": op_at(q)}, device_id_type=MESH)
    pl.semaphore_signal(barrier, inc=1, device_id={"sec": mate}, device_id_type=MESH)

    @pl.loop(1, groups)
    def _(d):
        pl.semaphore_signal(barrier, inc=1, device_id={"sec": ((g + d) % groups) * 2 + core}, device_id_type=MESH)

    load_r.start()
    load_l.start()

    def inside():
        row_ids = j * rows + lax.broadcasted_iota(jnp.int32, (rows, cols), 0)
        col_ids = lax.broadcasted_iota(jnp.int32, (rows, cols), 1)
        return (row_ids < dl_ref[0, 0]) & (col_ids < dr_ref[0, 0])

    psi = psi_ref[...]
    pan[0][0][s] = jnp.where(inside(), psi, jnp.zeros_like(psi))
    acc[...] = jnp.zeros_like(acc)

    pl.semaphore_wait(barrier, n_op - 1 + groups)

    def part_of(h, q):
        return pl.ds(sum(parts[q][:h]), parts[q][h])

    def z_copy(q, h):
        if q == high:
            src, dst, hop = pan[0][0].at[s, part_of(h, high)], pan[q][h].at[s], q
        elif q > high:
            src, dst, hop = pan[high][h].at[s], pan[q][0].at[s, part_of(h, high)], q - high
        else:
            src, dst, hop = pan[0][0].at[s, part_of(h, high)], pan[q][0].at[s, part_of(h, high)], q
        return pltpu.make_async_remote_copy(
            src_ref=src, dst_ref=dst, send_sem=z_send.at[q - 1, h], recv_sem=z_recv.at[q - 1, h],
            device_id={"op": op_at(hop)}, device_id_type=MESH)

    def s_copy(q, h, d, block):
        return pltpu.make_async_remote_copy(
            src_ref=pan[q][h].at[block], dst_ref=pan[q][h].at[block], send_sem=s_send.at[q, h, d - 1],
            recv_sem=s_recv.at[q, h, d - 1], device_id={"sec": ((g + d) % groups) * 2 + core}, device_id_type=MESH)

    def m_copy(q, h, d, block):
        return pltpu.make_async_remote_copy(
            src_ref=pan[q][h].at[block], dst_ref=pan[q][h].at[block], send_sem=m_send.at[q, h, d],
            recv_sem=m_recv.at[q, h, d], device_id={"sec": mate}, device_id_type=MESH)

    def x_copy(q, h, c):
        part = (pl.ds(c * per, per), part_of(h, q))
        return pltpu.make_async_remote_copy(
            src_ref=xs.at[(q - 1, *part)], dst_ref=xr.at[(q, *part)], send_sem=x_send.at[q - 1, h, c],
            recv_sem=x_recv.at[q - 1, h, c], device_id={"op": op_at(q)}, device_id_type=MESH)

    def r_copy(q, to):
        return pltpu.make_async_remote_copy(
            src_ref=sb.at[q, to - 1], dst_ref=rb.at[q, to - 1], send_sem=r_send.at[q, to - 1],
            recv_sem=r_recv.at[q, to - 1], device_id={"op": op_at(to)}, device_id_type=MESH)

    def near_copy(q):
        return pltpu.make_async_remote_copy(
            src_ref=near_out.at[q], dst_ref=near_in.at[q], send_sem=near_send.at[q], recv_sem=near_recv.at[q],
            device_id={"op": op_at(1)}, device_id_type=MESH)

    def far_copy(q):
        return pltpu.make_async_remote_copy(
            src_ref=far_out.at[q], dst_ref=far_in.at[q], send_sem=far_send.at[q], recv_sem=far_recv.at[q],
            device_id={"op": op_at(2)}, device_id_type=MESH)

    def spread(q, h):
        @pl.loop(1, groups)
        def _(d):
            s_copy(q, h, d, s).start()

        m_copy(q, h, 0, s).start()

    def collect(q, h):
        @pl.loop(1, groups)
        def _(d):
            block = from_group(d) * 2 + core
            s_copy(q, h, d, block).wait_recv()
            m_copy(q, h, d, block).start()

        @pl.loop(0, groups)
        def _(d):
            m_copy(q, h, d, from_group(d) * 2 + 1 - core).wait_recv()

    def images(q, h, c):
        @pl.loop(0, per, unroll=True)
        def _(i):
            k = c * per + i
            image = lax.dot_general(
                pan[q][h][src_ref[0, k]], rv[k], (((1,), (1,)), ((), ())), preferred_element_type=jnp.float32)
            image = jnp.where(k < cnt_ref[0, 0], image, jnp.zeros_like(image)).astype(jnp.bfloat16)
            if q:
                xs[q - 1, k, part_of(h, q)] = image
            else:
                xr[0, k, part_of(h, q)] = image

    def make(q):
        for h in range(len(parts[q])):
            collect(q, h)

            @pl.loop(0, chunks)
            def _(c):
                images(q, h, c)
                if q:
                    x_copy(q, h, c).start()

    pieces = range(len(parts[high]))
    for q in [high] + list(range(1, high)):
        for h in pieces:
            z_copy(q, h).start()
    for h in pieces:
        z_copy(high, h).wait_recv()
        spread(high, h)
        for q in range(high + 1, n_op):
            z_copy(q, h).start()
    load_r.wait()
    make(high)
    for q in order[1:]:
        for h in pieces:
            z_copy(q, h).wait_recv()
        spread(q, 0)
    spread(0, 0)
    for q in order[1:] + [0]:
        make(q)
    load_l.wait()

    def rows_of(q):
        return pl.ds(pl.multiple_of(op_at(q) * rows, rows), rows)

    gathered = []
    for q in [0] + order:
        @pl.loop(0, chunks)
        def _(c):
            if q:
                for h in range(len(parts[q])):
                    x_copy(q, h, c).wait_recv()
            lefts = jnp.concatenate([lv[c * per + i] for i in range(per)], axis=1)
            block = xr[q, pl.ds(c * per, per)].reshape(per * rows, width)
            acc[q] += jnp.dot(lefts, block, preferred_element_type=jnp.float32)

        gathered.append(q)
        if q in paired:
            for i, to in enumerate((1, 3)):
                near_out[q, i] = acc[q, rows_of(to), :].astype(near_out.dtype)
            near_copy(q).start()
            if flip(q, 1) in gathered:
                for p in (q, flip(q, 1)):
                    near_copy(flip(p, 1)).wait_recv()
                    both = acc[p, rows_of(2), :] + near_in[flip(p, 1), 1].astype(jnp.float32)
                    far_out[p] = both.astype(far_out.dtype)
                    far_copy(p).start()
            continue
        for to in order:
            sb[q, to - 1] = acc[q, rows_of(to), :].astype(sb.dtype)
            r_copy(q, to).start()

    def cols_of(q):
        return pl.ds(pl.multiple_of(op_at(q) * width, width), width)

    for q in [0] + order:
        total = acc[q, rows_of(0), :]
        if q in paired:
            total = total + near_in[flip(q, 1), 0].astype(jnp.float32)
        if flip(q, 2) in paired:
            far_copy(flip(q, 2)).wait_recv()
            total = total + far_in[flip(q, 2)].astype(jnp.float32)
        for to in order:
            if flip(q, to) in paired:
                continue
            r_copy(flip(q, to), to).wait_recv()
            total = total + rb[flip(q, to), to - 1].astype(jnp.float32)
        row_ids = j * rows + lax.broadcasted_iota(jnp.int32, (rows, width), 0)
        col_ids = op_at(q) * width + lax.broadcasted_iota(jnp.int32, (rows, width), 1)
        keep = (row_ids < dl_ref[0, 0]) & (col_ids < dr_ref[0, 0])
        out_ref[:, cols_of(q)] = jnp.where(keep, total, jnp.zeros_like(total)).astype(out_ref.dtype)

    for q in range(n_op):
        for h in range(len(parts[q])):
            @pl.loop(1, groups)
            def _(d):
                s_copy(q, h, d, s).wait_send()

            @pl.loop(0, groups)
            def _(d):
                m_copy(q, h, d, s).wait_send()

            if q:
                @pl.loop(0, chunks)
                def _(c):
                    x_copy(q, h, c).wait_send()

        if q in paired:
            near_copy(q).wait_send()
            far_copy(q).wait_send()
        else:
            for to in order:
                r_copy(q, to).wait_send()
        if q:
            for h in pieces:
                z_copy(q, h).wait_send()


def solution(mesh):
    n_sec, n_op = mesh.shape["sec"], mesh.shape["op"]

    def body(psi, left_ops, right_ops, sources, counts, dims_left, dims_right):
        rows, cols = psi.shape[1:]
        terms, _, height, depth = left_ops.shape
        width = right_ops.shape[2]
        groups = n_sec // 2
        chunks = max(c for c in range(1, 3) if terms % c == 0)
        parts = [(rows,)] * n_op
        parts[n_op // 2] = (rows // 4, rows - rows // 4)
        most = max(len(p) for p in parts)
        bf, dma = jnp.bfloat16, pltpu.SemaphoreType.DMA
        vmem, smem = pl.BlockSpec(memory_space=pltpu.VMEM), pl.BlockSpec(memory_space=pltpu.SMEM)
        hbm = pl.BlockSpec(memory_space=pl.ANY)
        out = pl.pallas_call(
            functools.partial(kernel, n_sec, n_op, chunks, parts),
            out_shape=jax.ShapeDtypeStruct((rows, cols), bf),
            in_specs=[vmem, hbm, hbm, smem, smem, smem, smem],
            out_specs=vmem,
            scratch_shapes=[pltpu.VMEM((n_sec, h, cols), bf) for p in parts for h in p] + [
                pltpu.VMEM((terms, height, depth), bf),
                pltpu.VMEM((terms, width, cols), bf),
                pltpu.VMEM((n_op - 1, terms, rows, width), bf),
                pltpu.VMEM((n_op, terms, rows, width), bf),
                pltpu.VMEM((n_op, height, width), jnp.float32),
                pltpu.VMEM((n_op, n_op - 1, rows, width), bf),
                pltpu.VMEM((n_op, n_op - 1, rows, width), bf),
                dma((2,)),
                dma((n_op - 1, most)), dma((n_op - 1, most)),
                dma((n_op, most, groups - 1)), dma((n_op, most, groups - 1)),
                dma((n_op, most, groups)), dma((n_op, most, groups)),
                dma((n_op - 1, most, chunks)), dma((n_op - 1, most, chunks)),
                dma((n_op, n_op - 1)), dma((n_op, n_op - 1)),
                pltpu.VMEM((n_op, 2, rows, width), bf), pltpu.VMEM((n_op, 2, rows, width), bf),
                pltpu.VMEM((n_op, rows, width), bf), pltpu.VMEM((n_op, rows, width), bf),
                dma((n_op,)), dma((n_op,)), dma((n_op,)), dma((n_op,)),
            ],
            compiler_params=pltpu.CompilerParams(
                collective_id=0, has_side_effects=True, vmem_limit_bytes=60 * 2**20),
        )(psi[0], left_ops[:, 0], right_ops[:, 0], sources, counts[None], dims_left[None], dims_right[None])
        return out[None]

    return jax.shard_map(
        body,
        mesh=mesh,
        in_specs=(
            P("sec", "op", None),
            P(None, "sec", None, "op"),
            P(None, "sec", "op", None),
            P("sec", None),
            P("sec"),
            P("sec"),
            P("sec"),
        ),
        out_specs=P("sec", "op", None),
        check_vma=False,
    )
```

profile of v0, /device:TPU:0, one launch (start us, length us, event | category | flops | bytes accessed | tf_op | source)
XLA Modules:
  0.0 99.0 jit_solution(3624906879632002003)
XLA Ops:
  1.9 95.5 %shard_map.73 = bf16[128,512]{1,0:T(8,128)(2,1)} custom-call(bf16[128,512]{1,0:T(8,128)(2,1)} %bitcast.13, bf16[24,512,128]{2,1,0:T(8,128)(2,1)} %bitcast.10, bf16[24,128,512]{2,1,0:T(8,128)(2,1)} %bitcast.11, s32[1,24]{1,0:T(1,128)} %src_ref.1, s32[1,1]{1,0:T(1,128)} %bitcast.7.cnt_ref, s32[1,1]{1,0:T(1,128)} %bitcast.8.dl_ref, s32[1,1]{1,0:T(1,128)} %bitcast.9.dr_ref), custom_call_target="tpu_custom_call" | custom-call | tf_op jit(solution)/shard_map/pallas_call | solution.py:269
  97.5 1.6 %copy.12 = bf16[1,128,512]{2,1,0:T(8,128)(2,1)} copy(bf16[1,128,512]{2,1,0:T(8,128)(2,1)} %bitcast.12) | data formatting | bytes 262144
where the time goes:
time: 99.2 us; the launch traced here: 99 us
  Pallas kernels  95.5 us (96%)
  between operations  1.95 us (2%)
  local copies, waits for them, and re-layouts  1.57 us (2%)
    pallas_call x1, Pallas kernels, body(): pl.pallas_call(functools.partial(kernel, n_sec, n_op, chunks, parts), out...  95.5 us

commit v1 on v0

--- a/solution.py
+++ b/solution.py
@@ -18,26 +18,28 @@
     return out + j // bit * bit
 
 
-def kernel(n_sec, n_op, chunks, parts, psi_ref, left_hbm, right_hbm, src_ref, cnt_ref, dl_ref, dr_ref, out_ref, *scratch):
+def kernel(n_sec, n_op, chunks, parts, psi_hbm, left_hbm, right_hbm, src_ref, cnt_ref, dl_ref, dr_ref, out_ref,
+           *scratch):
     pan, at = [], 0
     for q in range(n_op):
         pan.append(scratch[at:at + len(parts[q])])
         at += len(parts[q])
-    (lv, rv, xs, xr, acc, sb, rb, local_sem, z_send, z_recv, s_send, s_recv, m_send, m_recv, x_send, x_recv,
-     r_send, r_recv, near_out, near_in, far_out, far_in, near_send, near_recv, far_send, far_recv) = scratch[at:]
+    (psi_v, lv, rv, xs, xr, acc, local_sem, z_send, z_recv, s_send, s_recv, m_send, m_recv, x_send, x_recv,
+     near_out, near_in, far_out, far_in, near_send, near_recv, far_send, far_recv) = scratch[at:]
     s = lax.axis_index("sec")
     j = lax.axis_index("op")
     groups = n_sec // 2
     g, core = s // 2, s % 2
     mate = g * 2 + 1 - core
-    rows, cols = psi_ref.shape
+    rows, cols = psi_v.shape
     terms = lv.shape[0]
     width = rv.shape[1]
     per = terms // chunks
     high = n_op // 2
     order = [high] + list(range(1, high)) + list(range(high + 1, n_op))
-    paired = (0, 1, 2, 3) if n_op == 4 else ()
-
+    early, late = ((1, 2), (0, 3)) if n_op == 4 else ((), tuple(range(n_op)))
+
+    load_p = pltpu.make_async_copy(psi_hbm, psi_v, local_sem.at[2])
     load_r = pltpu.make_async_copy(right_hbm, rv, local_sem.at[0])
     load_l = pltpu.make_async_copy(left_hbm, lv, local_sem.at[1])
 
@@ -50,12 +52,14 @@
     barrier = pltpu.get_barrier_semaphore()
     for q in range(1, n_op):
         pl.semaphore_signal(barrier, inc=1, device_id={"op": op_at(q)}, device_id_type=MESH)
-    pl.semaphore_signal(barrier, inc=1, device_id={"sec": mate}, device_id_type=MESH)
 
     @pl.loop(1, groups)
     def _(d):
         pl.semaphore_signal(barrier, inc=1, device_id={"sec": ((g + d) % groups) * 2 + core}, device_id_type=MESH)
 
+    pl.semaphore_signal(barrier, inc=1, device_id={"sec": mate}, device_id_type=MESH)
+
+    load_p.start()
     load_r.start()
     load_l.start()
 
@@ -64,9 +68,11 @@
         col_ids = lax.broadcasted_iota(jnp.int32, (rows, cols), 1)
         return (row_ids < dl_ref[0, 0]) & (col_ids < dr_ref[0, 0])
 
-    psi = psi_ref[...]
-    pan[0][0][s] = jnp.where(inside(), psi, jnp.zeros_like(psi))
+    keep = inside()
     acc[...] = jnp.zeros_like(acc)
+    load_p.wait()
+    psi = psi_v[...]
+    pan[0][0][s] = jnp.where(keep, psi, jnp.zeros_like(psi))
 
     pl.semaphore_wait(barrier, n_op - 1 + groups)
 
@@ -100,20 +106,15 @@
             src_ref=xs.at[(q - 1, *part)], dst_ref=xr.at[(q, *part)], send_sem=x_send.at[q - 1, h, c],
             recv_sem=x_recv.at[q - 1, h, c], device_id={"op": op_at(q)}, device_id_type=MESH)
 
-    def r_copy(q, to):
-        return pltpu.make_async_remote_copy(
-            src_ref=sb.at[q, to - 1], dst_ref=rb.at[q, to - 1], send_sem=r_send.at[q, to - 1],
-            recv_sem=r_recv.at[q, to - 1], device_id={"op": op_at(to)}, device_id_type=MESH)
-
     def near_copy(q):
         return pltpu.make_async_remote_copy(
             src_ref=near_out.at[q], dst_ref=near_in.at[q], send_sem=near_send.at[q], recv_sem=near_recv.at[q],
             device_id={"op": op_at(1)}, device_id_type=MESH)
 
-    def far_copy(q):
-        return pltpu.make_async_remote_copy(
-            src_ref=far_out.at[q], dst_ref=far_in.at[q], send_sem=far_send.at[q], recv_sem=far_recv.at[q],
-            device_id={"op": op_at(2)}, device_id_type=MESH)
+    def far_copy(q, to):
+        return pltpu.make_async_remote_copy(
+            src_ref=far_out.at[q, to - 1], dst_ref=far_in.at[q, to - 1], send_sem=far_send.at[q, to - 1],
+            recv_sem=far_recv.at[q, to - 1], device_id={"op": op_at(to)}, device_id_type=MESH)
 
     def spread(q, h):
         @pl.loop(1, groups)
@@ -145,15 +146,14 @@
             else:
                 xr[0, k, part_of(h, q)] = image
 
-    def make(q):
-        for h in range(len(parts[q])):
-            collect(q, h)
-
-            @pl.loop(0, chunks)
-            def _(c):
-                images(q, h, c)
-                if q:
-                    x_copy(q, h, c).start()
+    def make(q, h):
+        collect(q, h)
+
+        @pl.loop(0, chunks)
+        def _(c):
+            images(q, h, c)
+            if q:
+                x_copy(q, h, c).start()
 
     pieces = range(len(parts[high]))
     for q in [high] + list(range(1, high)):
@@ -165,21 +165,24 @@
         for q in range(high + 1, n_op):
             z_copy(q, h).start()
     load_r.wait()
-    make(high)
+    for h in pieces:
+        make(high, h)
     for q in order[1:]:
         for h in pieces:
             z_copy(q, h).wait_recv()
         spread(q, 0)
     spread(0, 0)
     for q in order[1:] + [0]:
-        make(q)
+        make(q, 0)
     load_l.wait()
 
     def rows_of(q):
         return pl.ds(pl.multiple_of(op_at(q) * rows, rows), rows)
 
-    gathered = []
-    for q in [0] + order:
+    def swapped(to):
+        return flip(to, 1) - 1
+
+    def gather(q):
         @pl.loop(0, chunks)
         def _(c):
             if q:
@@ -189,37 +192,38 @@
             block = xr[q, pl.ds(c * per, per)].reshape(per * rows, width)
             acc[q] += jnp.dot(lefts, block, preferred_element_type=jnp.float32)
 
-        gathered.append(q)
-        if q in paired:
-            for i, to in enumerate((1, 3)):
-                near_out[q, i] = acc[q, rows_of(to), :].astype(near_out.dtype)
+    for q in early + late:
+        gather(q)
+        if q in early:
+            for to in range(1, n_op):
+                near_out[q, to - 1] = acc[q, rows_of(to), :].astype(near_out.dtype)
             near_copy(q).start()
-            if flip(q, 1) in gathered:
-                for p in (q, flip(q, 1)):
-                    near_copy(flip(p, 1)).wait_recv()
-                    both = acc[p, rows_of(2), :] + near_in[flip(p, 1), 1].astype(jnp.float32)
-                    far_out[p] = both.astype(far_out.dtype)
-                    far_copy(p).start()
             continue
-        for to in order:
-            sb[q, to - 1] = acc[q, rows_of(to), :].astype(sb.dtype)
-            r_copy(q, to).start()
+        if early:
+            near_copy(flip(q, 1)).wait_recv()
+        for to in reversed(range(1, n_op)):
+            total = acc[q, rows_of(to), :]
+            if early and to > 1:
+                total = total + near_in[flip(q, 1), swapped(to)].astype(jnp.float32)
+            far_out[q, to - 1] = total.astype(far_out.dtype)
+            far_copy(q, to).start()
 
     def cols_of(q):
         return pl.ds(pl.multiple_of(op_at(q) * width, width), width)
 
-    for q in [0] + order:
+    def take(q, to):
+        far_copy(flip(q, to), to).wait_recv()
+        return far_in[flip(q, to), to - 1].astype(jnp.float32)
+
+    for q in range(n_op):
         total = acc[q, rows_of(0), :]
-        if q in paired:
-            total = total + near_in[flip(q, 1), 0].astype(jnp.float32)
-        if flip(q, 2) in paired:
-            far_copy(flip(q, 2)).wait_recv()
-            total = total + far_in[flip(q, 2)].astype(jnp.float32)
-        for to in order:
-            if flip(q, to) in paired:
-                continue
-            r_copy(flip(q, to), to).wait_recv()
-            total = total + rb[flip(q, to), to - 1].astype(jnp.float32)
+        if not early:
+            for to in range(1, n_op):
+                total = total + take(q, to)
+        elif q in early:
+            total = total + take(q, 1) + take(q, 2)
+        else:
+            total = total + near_in[flip(q, 1), 0].astype(jnp.float32) + take(q, 3)
         row_ids = j * rows + lax.broadcasted_iota(jnp.int32, (rows, width), 0)
         col_ids = op_at(q) * width + lax.broadcasted_iota(jnp.int32, (rows, width), 1)
         keep = (row_ids < dl_ref[0, 0]) & (col_ids < dr_ref[0, 0])
@@ -240,12 +244,11 @@
                 def _(c):
                     x_copy(q, h, c).wait_send()
 
-        if q in paired:
+        if q in early:
             near_copy(q).wait_send()
-            far_copy(q).wait_send()
         else:
-            for to in order:
-                r_copy(q, to).wait_send()
+            for to in range(1, n_op):
+                far_copy(q, to).wait_send()
         if q:
             for h in pieces:
                 z_copy(q, h).wait_send()
@@ -269,25 +272,23 @@
         out = pl.pallas_call(
             functools.partial(kernel, n_sec, n_op, chunks, parts),
             out_shape=jax.ShapeDtypeStruct((rows, cols), bf),
-            in_specs=[vmem, hbm, hbm, smem, smem, smem, smem],
+            in_specs=[hbm, hbm, hbm, smem, smem, smem, smem],
             out_specs=vmem,
             scratch_shapes=[pltpu.VMEM((n_sec, h, cols), bf) for p in parts for h in p] + [
+                pltpu.VMEM((rows, cols), bf),
                 pltpu.VMEM((terms, height, depth), bf),
                 pltpu.VMEM((terms, width, cols), bf),
                 pltpu.VMEM((n_op - 1, terms, rows, width), bf),
                 pltpu.VMEM((n_op, terms, rows, width), bf),
                 pltpu.VMEM((n_op, height, width), jnp.float32),
-                pltpu.VMEM((n_op, n_op - 1, rows, width), bf),
-                pltpu.VMEM((n_op, n_op - 1, rows, width), bf),
-                dma((2,)),
+                dma((3,)),
                 dma((n_op - 1, most)), dma((n_op - 1, most)),
                 dma((n_op, most, groups - 1)), dma((n_op, most, groups - 1)),
                 dma((n_op, most, groups)), dma((n_op, most, groups)),
                 dma((n_op - 1, most, chunks)), dma((n_op - 1, most, chunks)),
-                dma((n_op, n_op - 1)), dma((n_op, n_op - 1)),
-                pltpu.VMEM((n_op, 2, rows, width), bf), pltpu.VMEM((n_op, 2, rows, width), bf),
-                pltpu.VMEM((n_op, rows, width), bf), pltpu.VMEM((n_op, rows, width), bf),
-                dma((n_op,)), dma((n_op,)), dma((n_op,)), dma((n_op,)),
+                pltpu.VMEM((n_op, n_op - 1, rows, width), bf), pltpu.VMEM((n_op, n_op - 1, rows, width), bf),
+                pltpu.VMEM((n_op, n_op - 1, rows, width), bf), pltpu.VMEM((n_op, n_op - 1, rows, width), bf),
+                dma((n_op,)), dma((n_op,)), dma((n_op, n_op - 1)), dma((n_op, n_op - 1)),
             ],
             compiler_params=pltpu.CompilerParams(
                 collective_id=0, has_side_effects=True, vmem_limit_bytes=60 * 2**20),

time: 99.2 us -> 98.5 us (level)
  no operation moved by 1% of the time
where the time goes in v1:
time: 98.5 us; the launch traced here: 98.3 us
  Pallas kernels  94.8 us (96%)
  between operations  1.95 us (2%)
  local copies, waits for them, and re-layouts  1.57 us (2%)
    pallas_call x1, Pallas kernels, body(): pl.pallas_call(functools.partial(kernel, n_sec, n_op, chunks, parts), out...  94.8 us

profile of v1, /device:TPU:0, one launch (start us, length us, event | category | flops | bytes accessed | tf_op | source)
XLA Modules:
  0.0 98.3 jit_solution(3127618295569916033)
XLA Ops:
  1.9 94.8 %shard_map.73 = bf16[128,512]{1,0:T(8,128)(2,1)} custom-call(bf16[128,512]{1,0:T(8,128)(2,1)} %bitcast.13, bf16[24,512,128]{2,1,0:T(8,128)(2,1)} %bitcast.10, bf16[24,128,512]{2,1,0:T(8,128)(2,1)} %bitcast.11, s32[1,24]{1,0:T(1,128)} %src_ref.1, s32[1,1]{1,0:T(1,128)} %bitcast.7.cnt_ref, s32[1,1]{1,0:T(1,128)} %bitcast.8.dl_ref, s32[1,1]{1,0:T(1,128)} %bitcast.9.dr_ref), custom_call_target="tpu_custom_call" | custom-call | tf_op jit(solution)/shard_map/pallas_call | solution.py:272
  96.8 1.6 %copy.12 = bf16[1,128,512]{2,1,0:T(8,128)(2,1)} copy(bf16[1,128,512]{2,1,0:T(8,128)(2,1)} %bitcast.12) | data formatting | bytes 262144

commit v2 on v1

--- a/solution.py
+++ b/solution.py
@@ -37,7 +37,10 @@
     per = terms // chunks
     high = n_op // 2
     order = [high] + list(range(1, high)) + list(range(high + 1, n_op))
-    early, late = ((1, 2), (0, 3)) if n_op == 4 else ((), tuple(range(n_op)))
+    early, late = ((2, 1), (0, 3)) if n_op == 4 else ((), tuple(range(n_op)))
+
+    inner = j // 2 != j % 2
+    hold = chunks * 2 // 4
 
     load_p = pltpu.make_async_copy(psi_hbm, psi_v, local_sem.at[2])
     load_r = pltpu.make_async_copy(right_hbm, rv, local_sem.at[0])
@@ -66,7 +69,7 @@
     def inside():
         row_ids = j * rows + lax.broadcasted_iota(jnp.int32, (rows, cols), 0)
         col_ids = lax.broadcasted_iota(jnp.int32, (rows, cols), 1)
-        return (row_ids < dl_ref[0, 0]) & (col_ids < dr_ref[0, 0])
+        return (row_ids < dl_ref[0]) & (col_ids < dr_ref[0])
 
     keep = inside()
     acc[...] = jnp.zeros_like(acc)
@@ -140,7 +143,7 @@
             k = c * per + i
             image = lax.dot_general(
                 pan[q][h][src_ref[0, k]], rv[k], (((1,), (1,)), ((), ())), preferred_element_type=jnp.float32)
-            image = jnp.where(k < cnt_ref[0, 0], image, jnp.zeros_like(image)).astype(jnp.bfloat16)
+            image = jnp.where(k < cnt_ref[0], image, jnp.zeros_like(image)).astype(jnp.bfloat16)
             if q:
                 xs[q - 1, k, part_of(h, q)] = image
             else:
@@ -152,7 +155,11 @@
         @pl.loop(0, chunks)
         def _(c):
             images(q, h, c)
-            if q:
+            if early and q == late[-1]:
+                @pl.when(inner)
+                def _():
+                    x_copy(q, h, c).start()
+            elif q:
                 x_copy(q, h, c).start()
 
     pieces = range(len(parts[high]))
@@ -164,10 +171,14 @@
         spread(high, h)
         for q in range(high + 1, n_op):
             z_copy(q, h).start()
+    for q in range(1, high):
+        for h in pieces:
+            z_copy(q, h).wait_recv()
+        spread(q, 0)
     load_r.wait()
     for h in pieces:
         make(high, h)
-    for q in order[1:]:
+    for q in range(high + 1, n_op):
         for h in pieces:
             z_copy(q, h).wait_recv()
         spread(q, 0)
@@ -192,7 +203,33 @@
             block = xr[q, pl.ds(c * per, per)].reshape(per * rows, width)
             acc[q] += jnp.dot(lefts, block, preferred_element_type=jnp.float32)
 
+    def resume(first, end):
+        @pl.when(jnp.logical_not(inner))
+        def _():
+            @pl.loop(first, end)
+            def _(c):
+                x_copy(late[-1], 0, c).start()
+
     for q in early + late:
+        if early and q == late[0]:
+            resume(0, hold)
+        if early and q == late[-1]:
+            resume(hold, chunks)
+        if q == late[-1]:
+            for q in range(n_op):
+                for h in range(len(parts[q])):
+                    @pl.loop(1, groups)
+                    def _(d):
+                        s_copy(q, h, d, s).wait_send()
+
+                    @pl.loop(0, groups)
+                    def _(d):
+                        m_copy(q, h, d, s).wait_send()
+
+                if q:
+                    for h in pieces:
+                        z_copy(q, h).wait_send()
+
         gather(q)
         if q in early:
             for to in range(1, n_op):
@@ -226,19 +263,11 @@
             total = total + near_in[flip(q, 1), 0].astype(jnp.float32) + take(q, 3)
         row_ids = j * rows + lax.broadcasted_iota(jnp.int32, (rows, width), 0)
         col_ids = op_at(q) * width + lax.broadcasted_iota(jnp.int32, (rows, width), 1)
-        keep = (row_ids < dl_ref[0, 0]) & (col_ids < dr_ref[0, 0])
+        keep = (row_ids < dl_ref[0]) & (col_ids < dr_ref[0])
         out_ref[:, cols_of(q)] = jnp.where(keep, total, jnp.zeros_like(total)).astype(out_ref.dtype)
 
     for q in range(n_op):
         for h in range(len(parts[q])):
-            @pl.loop(1, groups)
-            def _(d):
-                s_copy(q, h, d, s).wait_send()
-
-            @pl.loop(0, groups)
-            def _(d):
-                m_copy(q, h, d, s).wait_send()
-
             if q:
                 @pl.loop(0, chunks)
                 def _(c):
@@ -249,10 +278,6 @@
         else:
             for to in range(1, n_op):
                 far_copy(q, to).wait_send()
-        if q:
-            for h in pieces:
-                z_copy(q, h).wait_send()
-
 
 def solution(mesh):
     n_sec, n_op = mesh.shape["sec"], mesh.shape["op"]
@@ -262,7 +287,7 @@
         terms, _, height, depth = left_ops.shape
         width = right_ops.shape[2]
         groups = n_sec // 2
-        chunks = max(c for c in range(1, 3) if terms % c == 0)
+        chunks = max(c for c in range(1, 5) if terms % c == 0)
         parts = [(rows,)] * n_op
         parts[n_op // 2] = (rows // 4, rows - rows // 4)
         most = max(len(p) for p in parts)
@@ -271,7 +296,7 @@
         hbm = pl.BlockSpec(memory_space=pl.ANY)
         out = pl.pallas_call(
             functools.partial(kernel, n_sec, n_op, chunks, parts),
-            out_shape=jax.ShapeDtypeStruct((rows, cols), bf),
+            out_shape=pltpu.VMEM((rows, cols), bf),
             in_specs=[hbm, hbm, hbm, smem, smem, smem, smem],
             out_specs=vmem,
             scratch_shapes=[pltpu.VMEM((n_sec, h, cols), bf) for p in parts for h in p] + [
@@ -292,7 +317,7 @@
             ],
             compiler_params=pltpu.CompilerParams(
                 collective_id=0, has_side_effects=True, vmem_limit_bytes=60 * 2**20),
-        )(psi[0], left_ops[:, 0], right_ops[:, 0], sources, counts[None], dims_left[None], dims_right[None])
+        )(psi[0], left_ops[:, 0], right_ops[:, 0], sources, counts, dims_left, dims_right)
         return out[None]
 
     return jax.shard_map(

time: 98.5 us -> 96.3 us (0.978)
  Pallas kernels: 94.8 us -> 93.5 us
    pallas_call x1, Pallas kernels: 94.8 us -> 93.5 us  [body(): pl.pallas_call(functools.partial(kernel, n_sec, n_op, chunks, parts), out...]
where the time goes in v2:
time: 96.3 us; the launch traced here: 96.1 us
  Pallas kernels  93.5 us (97%)
  between operations  1.95 us (2%)
    pallas_call x1, Pallas kernels, body(): pl.pallas_call(functools.partial(kernel, n_sec, n_op, chunks, parts), out...  93.5 us

profile of v2, /device:TPU:0, one launch (start us, length us, event | category | flops | bytes accessed | tf_op | source)
XLA Modules:
  0.0 96.1 jit_solution(7314842459856987728)
XLA Ops:
  1.9 93.5 %shard_map.73 = bf16[128,512]{1,0:T(8,128)(2,1)S(1)} custom-call(bf16[128,512]{1,0:T(8,128)(2,1)} %bitcast.7, bf16[24,512,128]{2,1,0:T(8,128)(2,1)} %bitcast.5, bf16[24,128,512]{2,1,0:T(8,128)(2,1)} %bitcast.6, s32[1,24]{1,0:T(1,128)} %src_ref.1, s32[1]{0:T(128)S(6)} %copy.10.cnt_ref, s32[1]{0:T(128)S(6)} %copy.11.dl_ref, s32[1]{0:T(128)S(6)} %copy.12.dr_ref), custom_call_target="tpu_custom_call" | custom-call | tf_op jit(solution)/shard_map/pallas_call | solution.py:297
  95.5 0.7 copy.9
